TPU v7x, 256 devices: a whole 4x4x8 slice. The times are simulated.
256 devices in a mesh: wide: 16 (over x, y_lo, core), loop: 16 (over y_hi, z).
Axes of the slice: x: 4, y: 4 (y_hi: 2, y_lo: 2; y = y_hi * 2 + y_lo), z: 8, core: 2. Of those that a mesh axis runs over, the one named last changes fastest.
Arguments:
- query_grads: bfloat16 [65536, 16384], P('loop', 'wide'), may hold values from -6 to 6
- train_grads: bfloat16 [640, 16384], P('loop', 'wide'), may hold values from -0.046875 to 0.046875
- precond: bfloat16 [2048, 16384], P(None, 'wide'), may hold values from -3 to 3
Outputs:
- scores: float32 [65536, 640], P(('loop', 'wide'))
All inputs are finite; a program needn't handle non-finite values.
Results may differ from a plain program's by a relative error of at most 0.0029.
Values may be sent and summed in bfloat16 or wider, within the bound.
No kernel may reach another device: no remote copies, remote signals or barrier semaphores. Data moves between devices by JAX's collectives and lax.ppermute only.
A program may use at most 128 MiB of HBM per device.

v0:
```python
import jax
import jax.numpy as jnp
from jax import lax
from jax.sharding import PartitionSpec as P


def partner_2(block, axis, bit):
    count = lax.axis_size(axis)
    route = []
    for low in range(count):
        high = low | 1 << bit
        if high != low and high < count:
            route += [(low, high), (high, low)]
    return lax.ppermute(block, axis, route)


def contract_features(left_rows, right_rows):
    return lax.dot_general(
        left_rows, right_rows, (((1,), (1,)), ((), ())), preferred_element_type=jnp.float32
    )


def shards(query_grads, train_grads, precond):
    current = train_grads
    position = lax.axis_index("wide")
    partner = partner_2(current, "wide", 0)
    is_upper = position // 2**0 % 2
    current = jnp.where(
        is_upper == 1,
        jnp.concatenate([partner, current], axis=1),
        jnp.concatenate([current, partner], axis=1),
    )
    conditioned = jnp.dot(current, precond, preferred_element_type=jnp.float32).astype(jnp.bfloat16)
    owned_rows = lax.all_to_all(query_grads, "wide", split_axis=0, concat_axis=1, tiled=True)
    full_width = lax.all_gather(conditioned, "wide", axis=1, tiled=True)
    return contract_features(owned_rows, lax.all_gather(full_width, "loop", axis=0, tiled=True))


def solution(mesh):
    return jax.shard_map(
        shards,
        mesh=mesh,
        in_specs=(P("loop", "wide"), P("loop", "wide"), P(None, "wide")),
        out_specs=P(("loop", "wide"), None),
        check_vma=False,
    )
```

profile of v0, /device:TPU:1, one launch (start us, length us, event | category | flops | bytes accessed | tf_op | source)
XLA Modules:
  0.0 419.7 jit_solution(9244328703946631897)
XLA Ops:
  6.5 0.0 all-gather.3.cloned.1.call-start
  6.5 3.2 collective-permute-start
  9.8 1.1 collective-permute-done
  10.9 3.7 convolution_convert_fusion
  14.7 0.0 all-gather.3.cloned.1.call-update
  14.7 0.0 all-gather.5.cloned.1.call-start
  14.7 36.8 %all-gather.3.cloned.1.call-done = bf16[40,16384]{1,0:T(8,128)(2,1)} async-done(((bf16[40,1024]{1,0:T(8,128)(2,1)}), bf16[40,16384]{1,0:T(8,128)(2,1)}) %all-gather.3.cloned.1.call-update) | async-done | bytes 1310736 | tf_op jit(solution)/shard_map/all_gather | solution.py:35
  51.5 0.0 all-gather.5.cloned.1.call-update
  51.5 111.3 %all_to_all.19 = bf16[16,256,1024]{2,1,0:T(8,128)(2,1)} all-to-all(bf16[16,256,1024]{2,1,0:T(8,128)(2,1)} %bitcast.9), channel_id=1, replica_groups=mesh['wide'=16,'loop'=16] {'wide'}, dimensions={0} | all-to-all | bytes 16777216 | tf_op jit(solution)/shard_map/all_to_all | solution.py:34
  162.8 12.3 %copy.6 = bf16[256,16,1024]{0,2,1:T(8,128)(2,1)} copy(bf16[256,16,1024]{2,0,1:T(8,128)(2,1)} %bitcast.8) | data formatting | bytes 16777216 | tf_op jit(solution)/shard_map/all_to_all | solution.py:34
  175.1 224.4 %all-gather.5.cloned.1.call-done = bf16[640,16384]{1,0:T(8,128)(2,1)} async-done(((bf16[40,16384]{1,0:T(8,128)(2,1)}), bf16[640,16384]{1,0:T(8,128)(2,1)}) %all-gather.5.cloned.1.call-update) | async-done | bytes 20971536 | tf_op jit(solution)/shard_map/all_gather | solution.py:36
  399.5 12.2 %convolution_bitcast_fusion = f32[256,640]{0,1:T(8,128)S(1)} fusion(bf16[640,16384]{1,0:T(8,128)(2,1)} %all-gather.5.cloned.1.call-done, bf16[256,16384]{0,1:T(8,128)(2,1)} %bitcast.10), kind=kOutput, calls=%fused_computation | convolution fusion | flops 5368709120 | bytes 30015488 | tf_op jit(solution)/shard_map/dot_general | solution.py:18
  411.8 1.1 copy.7
Async XLA Ops:
  6.5 45.0 %all-gather.3.cloned.1.call-start = ((), (), s32[]{:S(2)}) async-start(), calls=%async_computation.1 | async-start | bytes 1392640 | tf_op jit(solution)/shard_map/all_gather | solution.py:35
  6.5 4.4 %collective-permute-start = (bf16[40,1024]{1,0:T(8,128)(2,1)}, bf16[40,1024]{1,0:T(8,128)(2,1)S(1)}, u32[]{:S(2)}, u32[]{:S(2)}) collective-permute-start(bf16[40,1024]{1,0:T(8,128)(2,1)} %param.4), channel_id=1, source_target_pairs={{0,16},{16,0},{32,48},{48,32},{64,80},{80,64},{96,112},{112,96},{1... | collective-permute-start | bytes 245768 | tf_op jit(solution)/shard_map/ppermute | solution.py:14
  14.7 384.9 %all-gather.5.cloned.1.call-start = ((), (), s32[]{:S(2)}) async-start(), calls=%async_computation.2 | async-start | bytes 22282240 | tf_op jit(solution)/shard_map/all_gather | solution.py:36
Sparse Core Ops, SparseCore 0:
  14.8 36.6 all-gather.2
  54.1 345.4 all-gather.4
where the time goes:
time: 420 us
  waiting for transfers between devices  262 us (62%)
  blocking collectives  111 us (26%)
  matrix products  16 us (4%)
  local copies, waits for them, and re-layouts  13.4 us (3%)
  between operations  13.4 us (3%)
    all_gather x1, waiting for transfers between devices, shards(): lax.all_gather(full_width, 'loop', axis=0, tiled=True)  224 us
    all_to_all x1, blocking collectives, shards(): lax.all_to_all(query_grads, 'wide', split_axis=0, concat_axis=1, tiled=True)  111 us
    all_gather x1, waiting for transfers between devices, shards(): full_width = lax.all_gather(conditioned, 'wide', axis=1, tiled=True)  36.8 us
    all_to_all x1, local copies, waits for them, and re-layouts, shards(): lax.all_to_all(query_grads, 'wide', split_axis=0, concat_axis=1, tiled=True)  12.3 us
    dot_general x1, matrix products, contract_features(): lax.dot_general(left_rows, right_rows, (((1,), (1,)), ((), ())), preferre...  12.2 us
  transfers between devices with their start and end apart: 3, of which 3 were waited for; matrix products, arithmetic and copies ran while one was open for 3% of the time, Pallas kernels for 0%

commit v1 on v0

--- a/solution.py
+++ b/solution.py
@@ -32,7 +32,9 @@
     )
     conditioned = jnp.dot(current, precond, preferred_element_type=jnp.float32).astype(jnp.bfloat16)
     owned_rows = lax.all_to_all(query_grads, "wide", split_axis=0, concat_axis=1, tiled=True)
-    full_width = lax.all_gather(conditioned, "wide", axis=1, tiled=True)
+    full_width = jnp.concatenate(
+        lax.all_to_all(jnp.stack([conditioned] * lax.axis_size("wide")), "wide", 0, 0), axis=1
+    )
     return contract_features(owned_rows, lax.all_gather(full_width, "loop", axis=0, tiled=True))
 
 

time: 420 us -> 407 us (0.969)
  waiting for transfers between devices: 262 us -> 227 us
  blocking collectives: 111 us -> 134 us
    all_gather x1 -> x0, waiting for transfers between devices: 36.8 us -> none  [shards(): full_width = lax.all_gather(conditioned, 'wide', axis=1, tiled=True)]
    all_to_all x0 -> x1, blocking collectives: none -> 22.4 us  [shards(): lax.all_to_all(jnp.stack([conditioned] * lax.axis_size('wide')), 'wide',...]
  transfers between devices with their start and end apart: 3 -> 2, of which waited for: 3 -> 2; matrix products, arithmetic and copies ran while one was open for 3% -> 3% of each run, Pallas kernels for 0% -> 0%
where the time goes in v1:
time: 407 us
  waiting for transfers between devices  227 us (56%)
  blocking collectives  134 us (33%)
  matrix products  15.3 us (4%)
  local copies, waits for them, and re-layouts  14.7 us (4%)
  between operations  13.4 us (3%)
    all_gather x1, waiting for transfers between devices, shards(): lax.all_gather(full_width, 'loop', axis=0, tiled=True)  225 us
    all_to_all x1, blocking collectives, shards(): lax.all_to_all(query_grads, 'wide', split_axis=0, concat_axis=1, tiled=True)  111 us
    all_to_all x1, blocking collectives, shards(): lax.all_to_all(jnp.stack([conditioned] * lax.axis_size('wide')), 'wide',...  22.4 us
    all_to_all x1, local copies, waits for them, and re-layouts, shards(): lax.all_to_all(query_grads, 'wide', split_axis=0, concat_axis=1, tiled=True)  12.3 us
    dot_general x1, matrix products, contract_features(): lax.dot_general(left_rows, right_rows, (((1,), (1,)), ((), ())), preferre...  12.2 us
  transfers between devices with their start and end apart: 2, of which 2 were waited for; matrix products, arithmetic and copies ran while one was open for 3% of the time, Pallas kernels for 0%

profile of v1, /device:TPU:1, one launch (start us, length us, event | category | flops | bytes accessed | tf_op | source)
XLA Modules:
  0.0 407.0 jit_solution(10554240596947327090)
XLA Ops:
  6.5 0.0 all-gather.2.cloned.1.call-start
  6.5 3.2 collective-permute-start
  9.8 1.1 collective-permute-done
  10.9 3.1 convolution_convert_fusion
  14.0 0.1 stack.2
  14.2 22.4 %all_to_all.24 = bf16[16,40,1024]{2,1,0:T(8,128)(2,1)S(1)} all-to-all(bf16[16,40,1024]{2,1,0:T(8,128)(2,1)S(1)} %stack.2), channel_id=1, replica_groups=mesh['wide'=16,'loop'=16] {'wide'}, dimensions={0} | all-to-all | bytes 2621440 | tf_op jit(solution)/shard_map/all_to_all | solution.py:36
  36.6 1.2 copy.11
  37.7 0.0 all-gather.2.cloned.1.call-update
  37.8 111.4 %all_to_all.25 = bf16[16,256,1024]{2,1,0:T(8,128)(2,1)} all-to-all(bf16[16,256,1024]{2,1,0:T(8,128)(2,1)} %bitcast.12), channel_id=1, replica_groups=mesh['wide'=16,'loop'=16] {'wide'}, dimensions={0} | all-to-all | bytes 16777216 | tf_op jit(solution)/shard_map/all_to_all | solution.py:34
  149.2 12.3 %copy.9 = bf16[256,16,1024]{0,2,1:T(8,128)(2,1)} copy(bf16[256,16,1024]{2,0,1:T(8,128)(2,1)} %bitcast.11) | data formatting | bytes 16777216 | tf_op jit(solution)/shard_map/all_to_all | solution.py:34
  161.4 225.4 %all-gather.2.cloned.1.call-done = bf16[640,16384]{1,0:T(8,128)(2,1)} async-done(((bf16[40,16384]{1,0:T(8,128)(2,1)}), bf16[640,16384]{1,0:T(8,128)(2,1)}) %all-gather.2.cloned.1.call-update) | async-done | bytes 20971536 | tf_op jit(solution)/shard_map/all_gather | solution.py:38
  386.8 12.2 %convolution_bitcast_fusion = f32[256,640]{0,1:T(8,128)S(1)} fusion(bf16[640,16384]{1,0:T(8,128)(2,1)} %all-gather.2.cloned.1.call-done, bf16[256,16384]{0,1:T(8,128)(2,1)} %bitcast.13), kind=kOutput, calls=%fused_computation | convolution fusion | flops 5368709120 | bytes 30015488 | tf_op jit(solution)/shard_map/dot_general | solution.py:18
  399.1 1.1 copy.10
Async XLA Ops:
  6.5 380.3 %all-gather.2.cloned.1.call-start = ((), (), s32[]{:S(2)}) async-start(), calls=%async_computation.2 | async-start | bytes 22282240 | tf_op jit(solution)/shard_map/all_gather | solution.py:38
  6.5 4.4 %collective-permute-start = (bf16[40,1024]{1,0:T(8,128)(2,1)}, bf16[40,1024]{1,0:T(8,128)(2,1)S(1)}, u32[]{:S(2)}, u32[]{:S(2)}) collective-permute-start(bf16[40,1024]{1,0:T(8,128)(2,1)} %param.4), channel_id=1, source_target_pairs={{0,16},{16,0},{32,48},{48,32},{64,80},{80,64},{96,112},{112,96},{1... | collective-permute-start | bytes 245768 | tf_op jit(solution)/shard_map/ppermute | solution.py:14
Sparse Core Ops, SparseCore 0:
  37.9 348.8 all-gather.1

commit v2 on v0

--- a/solution.py
+++ b/solution.py
@@ -31,7 +31,12 @@
         jnp.concatenate([current, partner], axis=1),
     )
     conditioned = jnp.dot(current, precond, preferred_element_type=jnp.float32).astype(jnp.bfloat16)
-    owned_rows = lax.all_to_all(query_grads, "wide", split_axis=0, concat_axis=1, tiled=True)
+    owned_rows = jnp.concatenate(
+        lax.all_to_all(
+            jnp.stack(jnp.split(query_grads, lax.axis_size("wide"), axis=0)), "wide", 0, 0
+        ),
+        axis=1,
+    )
     full_width = lax.all_gather(conditioned, "wide", axis=1, tiled=True)
     return contract_features(owned_rows, lax.all_gather(full_width, "loop", axis=0, tiled=True))
 

time: 420 us -> 396 us (0.943)
  waiting for transfers between devices: 262 us -> 215 us
  local copies, waits for them, and re-layouts: 13.4 us -> 37.6 us
    all_gather x1, waiting for transfers between devices: 224 us -> 177 us  [shards(): lax.all_gather(full_width, 'loop', axis=0, tiled=True)]
    unnamed x0 -> x37, local copies, waits for them, and re-layouts: none -> 31.8 us
    all_to_all x1 -> x0, local copies, waits for them, and re-layouts: 12.3 us -> none  [shards(): lax.all_to_all(query_grads, 'wide', split_axis=0, concat_axis=1, tiled=True)]
    split x0 -> x1, local copies, waits for them, and re-layouts: none -> 5.79 us  [shards(): jnp.split(query_grads, lax.axis_size('wide'), axis=0)]
  transfers between devices with their start and end apart: 3 -> 3, of which waited for: 3 -> 3; matrix products, arithmetic and copies ran while one was open for 3% -> 10% of each run, Pallas kernels for 0% -> 0%
where the time goes in v2:
time: 396 us; the launch traced here: 395 us
  waiting for transfers between devices  215 us (54%)
  blocking collectives  108 us (27%)
  local copies, waits for them, and re-layouts  37.6 us (9%)
  matrix products  17.5 us (4%)
  between operations  13.6 us (3%)
    all_gather x1, waiting for transfers between devices, shards(): lax.all_gather(full_width, 'loop', axis=0, tiled=True)  177 us
    all_to_all x1, blocking collectives, shards(): lax.all_to_all(jnp.stack(jnp.split(query_grads, lax.axis_size('wide'), ax...  108 us
    all_gather x1, waiting for transfers between devices, shards(): full_width = lax.all_gather(conditioned, 'wide', axis=1, tiled=True)  36.8 us
    unnamed x37, local copies, waits for them, and re-layouts  31.8 us
    dot_general x1, matrix products, contract_features(): lax.dot_general(left_rows, right_rows, (((1,), (1,)), ((), ())), preferre...  13.7 us
  transfers between devices with their start and end apart: 3, of which 3 were waited for; matrix products, arithmetic and copies ran while one was open for 10% of the time, Pallas kernels for 0%

profile of v2, /device:TPU:1, one launch (start us, length us, event | category | flops | bytes accessed | tf_op | source)
XLA Modules:
  0.0 395.2 jit_solution(902701439008302278)
XLA Ops:
  6.5 3.2 collective-permute-start
  9.8 1.1 collective-permute-done
  10.9 3.7 convolution_convert_fusion
  14.7 36.8 %all-gather.3.cloned.1.call-done = bf16[40,16384]{1,0:T(8,128)(2,1)} async-done(((bf16[40,1024]{1,0:T(8,128)(2,1)}), bf16[40,16384]{1,0:T(8,128)(2,1)}) %all-gather.3.cloned.1.call-update) | async-done | bytes 1310736 | tf_op jit(solution)/shard_map/all_gather | solution.py:40
  51.5 5.8 %fusion.7 = (bf16[256,1024]{1,0:T(8,128)(2,1)S(1)}, bf16[256,1024]{1,0:T(8,128)(2,1)S(1)}, bf16[256,1024]{1,0:T(8,128)(2,1)S(1)}, bf16[256,1024]{1,0:T(8,128)(2,...) fusion(bf16[4096,1024]{1,0:T(8,128)(2,1)} %param.3), kind=kLoop, calls=%fused_computation.25 | loop fusion | bytes 16777216 | tf_op jit(solution)/shard_map/split | solution.py:36
  57.3 2.1 copy.20
  59.4 2.1 copy.21
  61.4 2.1 copy.22
  63.5 2.0 copy.23
  65.5 2.1 copy.24
  67.7 2.1 copy.25
  69.8 2.1 copy.26
  71.9 2.0 copy.27
  74.0 2.0 copy.28
  76.0 2.0 copy.29
  78.1 1.0 copy.30
  79.1 0.2 copy.31
  79.3 0.2 copy.32
  79.5 0.2 copy.33
  79.7 0.2 copy.34
  79.9 0.2 copy.35
  80.1 1.2 bitcast_dynamic-update-slice_fusion.15
  81.3 1.1 bitcast_dynamic-update-slice_fusion.14
  82.4 1.1 bitcast_dynamic-update-slice_fusion.13
  83.5 1.1 bitcast_dynamic-update-slice_fusion.12
  84.6 1.1 bitcast_dynamic-update-slice_fusion.11
  85.7 1.1 bitcast_dynamic-update-slice_fusion.10
  86.7 1.1 bitcast_dynamic-update-slice_fusion.9
  87.8 1.1 bitcast_dynamic-update-slice_fusion.8
  89.3 108.0 %all_to_all.5 = bf16[16,256,1024]{1,2,0:T(8,128)(2,1)} all-to-all(bf16[16,256,1024]{1,2,0:T(8,128)(2,1)S(1)} %bitcast_dynamic-update-slice_fusion), channel_id=1, replica_groups=mesh['wide'=16,'loop'=16] {'wide'}, dimensions={0} | all-to-all | bytes 16777216 | tf_op jit(solution)/shard_map/all_to_all | solution.py:35
  197.4 177.3 %all-gather.5.cloned.1.call-done = bf16[640,16384]{1,0:T(8,128)(2,1)} async-done(((bf16[40,16384]{1,0:T(8,128)(2,1)}), bf16[640,16384]{1,0:T(8,128)(2,1)}) %all-gather.5.cloned.1.call-update) | async-done | bytes 20971536 | tf_op jit(solution)/shard_map/all_gather | solution.py:41
  374.7 13.7 %fusion.8 = f32[256,640]{1,0:T(8,128)} fusion(bf16[256,16384]{0,1:T(8,128)(2,1)} %bitcast.38, bf16[640,16384]{1,0:T(8,128)(2,1)} %all-gather.5.cloned.1.call-done), kind=kOutput, calls=%fused_computation.26 | convolution fusion | flops 5368709120 | bytes 30015488 | tf_op jit(solution)/shard_map/dot_general | solution.py:18
  (18 shorter events, 0.4 us)
Async XLA Ops:
  6.5 45.0 %all-gather.3.cloned.1.call-start = ((), (), s32[]{:S(2)}) async-start(), calls=%async_computation.1 | async-start | bytes 1392640 | tf_op jit(solution)/shard_map/all_gather | solution.py:40
  6.5 4.4 %collective-permute-start = (bf16[40,1024]{1,0:T(8,128)(2,1)}, bf16[40,1024]{1,0:T(8,128)(2,1)S(1)}, u32[]{:S(2)}, u32[]{:S(2)}) collective-permute-start(bf16[40,1024]{1,0:T(8,128)(2,1)} %param.4), channel_id=1, source_target_pairs={{0,16},{16,0},{32,48},{48,32},{64,80},{80,64},{96,112},{112,96},{1... | collective-permute-start | bytes 245768 | tf_op jit(solution)/shard_map/ppermute | solution.py:14
  14.7 360.0 %all-gather.5.cloned.1.call-start = ((), (), s32[]{:S(2)}) async-start(), calls=%async_computation.2 | async-start | bytes 22282240 | tf_op jit(solution)/shard_map/all_gather | solution.py:41
  80.1 8.8 %copy-start.2 = (bf16[256,1024]{0,1:T(8,128)(2,1)S(1)}, bf16[256,1024]{0,1:T(8,128)(2,1)}, u32[]{:S(2)}) copy-start(bf16[256,1024]{0,1:T(8,128)(2,1)} %copy.28) | copy-start | bytes 1572868
  80.1 8.9 %copy-start.1 = (bf16[256,1024]{0,1:T(8,128)(2,1)S(1)}, bf16[256,1024]{0,1:T(8,128)(2,1)}, u32[]{:S(2)}) copy-start(bf16[256,1024]{0,1:T(8,128)(2,1)} %copy.29) | copy-start | bytes 1572868
  80.1 8.9 %copy-start = (bf16[256,1024]{0,1:T(8,128)(2,1)S(1)}, bf16[256,1024]{0,1:T(8,128)(2,1)}, u32[]{:S(2)}) copy-start(bf16[256,1024]{0,1:T(8,128)(2,1)} %copy.30) | copy-start | bytes 1572868
Sparse Core Ops, SparseCore 0:
  14.8 36.6 all-gather.2
  54.1 320.5 all-gather.4
